TPU v7x, 32 devices: a whole 2x2x4 slice. The times are simulated.
32 devices in a mesh: facet: 4 (over y, x), band: 4 (over z), sub: 2 (over core).
Axes of the slice: x: 2, y: 2, z: 4, core: 2. Of those that a mesh axis runs over, the one named last changes fastest.
Arguments:
- facets: bfloat16 [8192, 2048], P(('facet', 'band')), may hold values from -6 to 6
- window: float32 [2048], replicated, may hold values from 0.5 to 1.5
- facet_offsets: int32 [4, 2], replicated, may hold values from 0 to 49151
- row_offsets: int32 [8], replicated, may hold values from 0 to 49151
- column_offset: int32 [1], replicated, may hold values from 0 to 49151
- kernel: bfloat16 [256, 256], replicated, may hold values from -0.375 to 0.375
- tile_counts: int32 [8, 16, 16], replicated, may hold values from 0 to 32
Outputs:
- residual: bfloat16 [8192, 2048], P(('facet', 'band'))
All inputs are finite; a program needn't handle non-finite values.
Results may differ from a plain program's by a relative error of at most 0.013.
Values may be sent and summed in bfloat16 or wider, within the bound.
A program may use at most 64 MiB of HBM per device.

v0:
```python
import math
import jax
import jax.numpy as jnp
from jax import lax
from jax.sharding import PartitionSpec as P

IMAGE = 49152


def modular_product(first, second):
    upper_bits = first // 256
    lower_bits = first % 256
    reduced = upper_bits * second % IMAGE
    reduced = reduced * 256 % IMAGE
    return (reduced + lower_bits * second) % IMAGE


def phase_table(frequency, position):
    reduced = modular_product(frequency % IMAGE, position % IMAGE)
    angle = reduced.astype(jnp.float32) * (2.0 * math.pi / IMAGE)
    return (jnp.cos(angle), jnp.sin(angle))


def product(left, right):
    return jnp.dot(left, right, preferred_element_type=jnp.float32)


def body(facets, window, facet_offsets, row_offsets, column_offset, kernel, tile_counts):
    facet_count = lax.axis_size("facet")
    band_count = lax.axis_size("band")
    sub_count = lax.axis_size("sub")
    facet_at = lax.axis_index("facet")
    band_at = lax.axis_index("band")
    sub_at = lax.axis_index("sub")
    band_rows = facets.shape[0]
    width = facets.shape[1]
    contrib = kernel.shape[0]
    sub_rows = contrib // band_count
    stacked = band_count * contrib
    a_scale = 1.0 / math.sqrt(width * facet_count)
    b_scale = 1.0 / math.sqrt(width)
    back_scale = 1.0 / math.sqrt(band_count * sub_count * contrib)
    out_scale = 1.0 / math.sqrt(contrib)
    offset = lax.dynamic_slice_in_dim(facet_offsets, facet_at, 1, 0)[0]
    cells = jnp.arange(width, dtype=jnp.int32)
    frequencies = jnp.arange(contrib, dtype=jnp.int32)
    cosine, sine = phase_table(column_offset[0] + frequencies[:, None], offset[1] + cells[None, :])
    col_real = (cosine * window[None, :] * b_scale).astype(jnp.bfloat16)
    col_imag = (-sine * window[None, :] * b_scale).astype(jnp.bfloat16)
    t_real = jnp.einsum("xy,ky->xk", facets, col_real, preferred_element_type=jnp.float32).astype(
        jnp.bfloat16
    )
    t_imag = jnp.einsum("xy,ky->xk", facets, col_imag, preferred_element_type=jnp.float32).astype(
        jnp.bfloat16
    )
    starts = lax.dynamic_slice_in_dim(row_offsets, sub_at * band_count, band_count, 0)
    row_freqs = (starts[:, None] + frequencies[None, :]).reshape(stacked)
    positions = offset[0] + band_at * band_rows + jnp.arange(band_rows, dtype=jnp.int32)
    row_cos, row_sin = phase_table(row_freqs[:, None], positions[None, :])
    a_real = (row_cos * a_scale).astype(jnp.bfloat16)
    a_imag = (-row_sin * a_scale).astype(jnp.bfloat16)
    part_real = product(a_real, t_real) - product(a_imag, t_imag)
    part_imag = product(a_real, t_imag) + product(a_imag, t_real)
    terms = jnp.stack([part_real, part_imag]).reshape(2, band_count, band_count, sub_rows, contrib)
    blocks = lax.psum_scatter(
        terms.astype(jnp.bfloat16), "band", scatter_dimension=2, tiled=True
    ).astype(jnp.float32)
    blocks = lax.psum(blocks, "facet")
    grid_part = blocks.reshape(2, band_count, sub_rows, contrib).astype(jnp.bfloat16)
    tiles = tile_counts.shape[1]
    tile_side = contrib // tiles
    counts = lax.dynamic_slice_in_dim(tile_counts, sub_at * band_count, band_count, 0).astype(
        jnp.float32
    )
    ratio = counts / (counts + 4.0)
    weights = jnp.broadcast_to(
        ratio[:, :, None, :, None], (band_count, tiles, tile_side, tiles, tile_side)
    )
    weights = weights.reshape(band_count, contrib, contrib)
    y_cols = jnp.einsum(
        "ij,cgrj->cgir", kernel, grid_part, preferred_element_type=jnp.float32
    ).astype(jnp.bfloat16)
    y_cols = lax.all_to_all(y_cols, "band", split_axis=2, concat_axis=3, tiled=True)
    z_cols = jnp.einsum("cgqi,ji->cgqj", y_cols, kernel, preferred_element_type=jnp.float32)
    weight_cols = jnp.swapaxes(
        lax.dynamic_slice_in_dim(weights, band_at * sub_rows, sub_rows, 2), 1, 2
    )
    w_cols = (weight_cols[None] * z_cols).astype(jnp.bfloat16)
    u_cols = jnp.einsum("cgqj,jl->cgql", w_cols, kernel, preferred_element_type=jnp.float32).astype(
        jnp.bfloat16
    )
    u_back = lax.all_to_all(u_cols, "band", split_axis=3, concat_axis=2, tiled=True)
    residual_grid = jnp.einsum(
        "cgqr,qm->cgrm", u_back, kernel, preferred_element_type=jnp.float32
    ).astype(jnp.bfloat16)
    back_real = (row_cos * back_scale).astype(jnp.bfloat16).reshape(band_count, contrib, band_rows)
    back_imag = (row_sin * back_scale).astype(jnp.bfloat16).reshape(band_count, contrib, band_rows)
    piece = lax.all_gather(residual_grid, "band", axis=2, tiled=True)
    e_real = jnp.einsum("gkx,gkl->xl", back_real, piece[0], preferred_element_type=jnp.float32)
    e_real = e_real - jnp.einsum(
        "gkx,gkl->xl", back_imag, piece[1], preferred_element_type=jnp.float32
    )
    e_imag = jnp.einsum("gkx,gkl->xl", back_real, piece[1], preferred_element_type=jnp.float32)
    e_imag = e_imag + jnp.einsum(
        "gkx,gkl->xl", back_imag, piece[0], preferred_element_type=jnp.float32
    )
    e_real, e_imag = (e_real, e_imag)
    e_real, e_imag = (
        lax.psum(e_real.astype(jnp.bfloat16), "sub").astype(jnp.float32),
        lax.psum(e_imag.astype(jnp.bfloat16), "sub").astype(jnp.float32),
    )
    out_cos = (cosine * out_scale).astype(jnp.bfloat16)
    out_sin = (sine * out_scale).astype(jnp.bfloat16)
    image = product(e_real.astype(jnp.bfloat16), out_cos) - product(
        e_imag.astype(jnp.bfloat16), out_sin
    )
    return (window[None, :] * image).astype(jnp.bfloat16)


def solution(mesh):
    in_specs = (P(("facet", "band"), None), P(), P(), P(), P(), P(), P())
    out_specs = P(("facet", "band"), None)
    return jax.shard_map(body, mesh=mesh, in_specs=in_specs, out_specs=out_specs, check_vma=False)
```

profile of v0, /device:TPU:0, one launch (start us, length us, event | category | flops | bytes accessed | tf_op | source)
XLA Modules:
  0.0 311.3 jit_solution(18280598410825204298)
XLA Ops:
  7.3 0.8 constant_dynamic-slice_fusion
  8.1 0.5 fusion.138
  8.7 0.7 add_select_fusion.9
  9.3 12.9 %convolution_convert_fusion.3 = bf16[256,512]{1,0:T(8,128)(2,1)} fusion(bf16[512,2048]{1,0:T(8,128)(2,1)S(1)} %copy-done, f32[2048]{0:T(1024)} %param.8, s32[256]{0:T(256)S(1)} %get-tuple-element.14, s32[2048]{0:T(1024)S(1)} %add_select_fusion.9, s32[256]{0:T(256)S(1)} %get-tuple-element.15), kind=kOutput, calls=%fused_computation.73 | convolution fusion | flops 551682048 | bytes 2377728 | tf_op jit(solution)/shard_map/xy,ky->xk/dot_general | solution.py:53
  22.3 10.5 %convolution_convert_fusion.4 = bf16[256,512]{1,0:T(8,128)(2,1)S(1)} fusion(bf16[512,2048]{1,0:T(8,128)(2,1)S(1)} %copy-done, f32[2048]{0:T(1024)S(1)} %copy-done.11, s32[256]{0:T(256)S(1)} %get-tuple-element.14, s32[2048]{0:T(1024)S(1)} %add_select_fusion.9, s32[256]{0:T(256)S(1)} %get-tuple-element.15), kind=kOutput, calls=%fused_computation.74 | convolution fusion | flops 551157760 | bytes 2377728 | tf_op jit(solution)/shard_map/xy,ky->xk/dot_general | solution.py:50
  33.6 10.6 %fusion.58 = f32[1024,256]{1,0:T(8,128)S(1)} fusion(bf16[256,512]{1,0:T(8,128)(2,1)S(1)} %convolution_convert_fusion.4, s32[1024]{0:T(1024)S(1)} %get-tuple-element.8, s32[512]{0:T(512)S(1)} %add_select_fusion.16, s32[1024]{0:T(1024)S(1)} %get-tuple-element.7), kind=kOutput, calls=%fused_computation.88 | convolution fusion | flops 282066944 | bytes 1320960 | tf_op jit(solution)/shard_map/dot_general | solution.py:25
  44.2 10.7 %fusion.57 = f32[1024,256]{1,0:T(8,128)S(1)} fusion(bf16[256,512]{1,0:T(8,128)(2,1)S(1)} %copy-done.14, s32[1024]{0:T(1024)S(1)} %get-tuple-element.8, s32[512]{0:T(512)S(1)} %add_select_fusion.16, s32[1024]{0:T(1024)S(1)} %get-tuple-element.7), kind=kOutput, calls=%fused_computation.87 | convolution fusion | flops 282066944 | bytes 1320960 | tf_op jit(solution)/shard_map/dot_general | solution.py:25
  54.9 11.6 %fusion.36 = bf16[1024,256]{1,0:T(8,128)(2,1)S(1)} fusion(f32[1024,256]{1,0:T(8,128)S(1)} %fusion.58, bf16[256,512]{1,0:T(8,128)(2,1)S(1)} %copy-done.14, s32[1024]{0:T(1024)S(1)} %get-tuple-element.8, s32[512]{0:T(512)S(1)} %add_select_fusion.16, s32[1024]{0:T(1024)S(1)} %get-tuple-element.7), kind=kOutput, calls=%fused_computation.59 | convolution fusion | flops 283115520 | bytes 1845248 | tf_op jit(solution)/shard_map/dot_general | solution.py:25
  66.5 12.0 %fusion.37 = bf16[1024,256]{1,0:T(8,128)(2,1)S(1)} fusion(f32[1024,256]{1,0:T(8,128)S(1)} %fusion.57, bf16[256,512]{1,0:T(8,128)(2,1)S(1)} %convolution_convert_fusion.4, s32[1024]{0:T(1024)S(1)} %get-tuple-element.8, s32[512]{0:T(512)S(1)} %add_select_fusion.16, s32[1024]{0:T(1024)S(1)} %get-tuple-element.7), kind=kOutput, calls=%fused_computation.60 | convolution fusion | flops 283115520 | bytes 1845248 | tf_op jit(solution)/shard_map/dot_general | solution.py:25
  78.6 1.0 copy.25
  79.8 30.1 %reduce-scatter.2.cloned.1.call-done = bf16[2,4,1,64,256]{4,3,1,0,2:T(8,128)(2,1)} async-done(((bf16[2,4,4,64,256]{4,3,1,0,2:T(8,128)(2,1)}), bf16[2,4,1,64,256]{4,3,1,0,2:T(8,128)(2,1)}) %reduce-scatter.2.cloned.1.call-update) | async-done | bytes 262160 | tf_op jit(solution)/shard_map/reduce_scatter | solution.py:65
  109.9 44.5 %all-reduce.4.cloned.1.call-done = bf16[2,4,1,64,256]{4,3,1,0,2:T(8,128)(2,1)} async-done(((bf16[2,4,1,64,256]{4,3,1,0,2:T(8,128)(2,1)}), bf16[2,4,1,64,256]{4,3,1,0,2:T(8,128)(2,1)}) %all-reduce.4.cloned.1.call-update) | async-done | bytes 262160 | tf_op jit(solution)/shard_map/psum | solution.py:68
  154.4 1.2 fusion.43
  155.9 1.1 reshape.290
  157.0 4.6 %all-to-all-start = ((bf16[4,2,16384]{2,1,0:T(2,128)(2,1)}), bf16[4,2,16384]{2,1,0:T(2,128)(2,1)S(1)}, u32[]{:S(2)}, u32[]{:S(2)}) async-start(bf16[4,2,16384]{2,1,0:T(2,128)(2,1)} %reshape.290), calls=%async_computation.1 | async-start | bytes 524288 | tf_op jit(solution)/shard_map/all_to_all | solution.py:83
  161.7 3.9 %broadcast_in_dim.2 = f32[4,16,16,16,16]{2,1,4,3,0:T(8,128)} broadcast(f32[4,16,16]{1,2,0:T(8,128)S(1)} %copy.17), dimensions={0,1,3} | broadcast | bytes 1052672 | tf_op jit(solution)/shard_map/broadcast_in_dim | solution.py:76
  165.6 6.1 %reshape.284 = f32[4,256,256]{1,2,0:T(8,128)S(1)} reshape(f32[4,16,16,16,16]{2,1,4,3,0:T(8,128)} %broadcast_in_dim.2) | data formatting | bytes 2097152 | tf_op jit(solution)/shard_map/reshape | solution.py:79
  171.7 0.7 dynamic-slice_bitcast_fusion
  172.8 0.4 copy.30
  173.6 1.4 convolution_convert_fusion.1
  175.3 0.4 reshape.292
  175.7 12.7 %all_to_all.36 = bf16[4,2,16384]{2,1,0:T(2,128)(2,1)S(1)} all-to-all(bf16[4,2,16384]{2,1,0:T(2,128)(2,1)S(1)} %reshape.292), channel_id=1, replica_groups=mesh['facet'=4,'band'=4,'sub'=2] {'band'}, dimensions={0} | all-to-all | bytes 524288 | tf_op jit(solution)/shard_map/all_to_all | solution.py:92
  188.8 0.4 copy.29
  189.5 0.9 convolution_convert_fusion
  190.7 26.0 %all-gather.2.cloned.1.call-done = bf16[2,4,256,256]{3,2,1,0:T(8,128)(2,1)} async-done(((bf16[2,4,64,256]{3,2,1,0:T(8,128)(2,1)}), bf16[2,4,256,256]{3,2,1,0:T(8,128)(2,1)}) %all-gather.2.cloned.1.call-update) | async-done | bytes 1048592 | tf_op jit(solution)/shard_map/all_gather | solution.py:98
  216.7 11.7 %convolution_bitcast_fusion = f32[512,256]{1,0:T(8,128)S(1)} fusion(s32[4,256]{1,0:T(4,128)S(1)} %get-tuple-element.12, s32[512]{0:T(512)S(1)} %copy-done.4, s32[4,256]{1,0:T(4,128)S(1)} %get-tuple-element.13, bf16[2,4,256,256]{3,2,1,0:T(8,128)(2,1)} %all-gather.2.cloned.1.call-done), kind=kOutput, calls=%fused_computation.61 | convolution fusion | flops 282066944 | bytes 1058816 | tf_op jit(solution)/shard_map/gkx,gkl->xl/dot_general | solution.py:104
  228.4 10.8 %convolution_bitcast_fusion.2 = f32[512,256]{1,0:T(8,128)S(1)} fusion(s32[4,256]{1,0:T(4,128)S(1)} %get-tuple-element.12, s32[512]{0:T(512)S(1)} %copy-done.4, s32[4,256]{1,0:T(4,128)S(1)} %get-tuple-element.13, bf16[2,4,256,256]{3,2,1,0:T(8,128)(2,1)S(1)} %copy-done.9), kind=kOutput, calls=%fused_computation.63 | convolution fusion | flops 282066944 | bytes 1058816 | tf_op jit(solution)/shard_map/gkx,gkl->xl/dot_general | solution.py:100
  239.2 11.6 %fusion.40 = bf16[512,256]{1,0:T(8,128)(2,1)} fusion(f32[512,256]{1,0:T(8,128)S(1)} %convolution_bitcast_fusion, s32[4,256]{1,0:T(4,128)S(1)} %get-tuple-element.12, s32[512]{0:T(512)S(1)} %copy-done.4, s32[4,256]{1,0:T(4,128)S(1)} %get-tuple-element.13, bf16[2,4,256,256]{3,2,1,0:T(8,128)(2,1)S(1)} %copy-done.9), kind=kOutput, calls=%fused_computation.68 | convolution fusion | flops 282329088 | bytes 1320960 | tf_op jit(solution)/shard_map/gkx,gkl->xl/dot_general | solution.py:103
  250.7 11.4 %fusion.41 = bf16[512,256]{1,0:T(8,128)(2,1)} fusion(f32[512,256]{1,0:T(8,128)S(1)} %convolution_bitcast_fusion.2, s32[4,256]{1,0:T(4,128)S(1)} %get-tuple-element.12, s32[512]{0:T(512)S(1)} %copy-done.4, s32[4,256]{1,0:T(4,128)S(1)} %get-tuple-element.13, bf16[2,4,256,256]{3,2,1,0:T(8,128)(2,1)S(1)} %copy-done.9), kind=kOutput, calls=%fused_computation.69 | convolution fusion | flops 282329088 | bytes 1320960 | tf_op jit(solution)/shard_map/gkx,gkl->xl/dot_general | solution.py:99
  262.1 18.2 %all-reduce.6.cloned.1.call-done = (bf16[512,256]{1,0:T(8,128)(2,1)}, bf16[512,256]{1,0:T(8,128)(2,1)}) async-done(((bf16[512,256]{1,0:T(8,128)(2,1)}, bf16[512,256]{1,0:T(8,128)(2,1)}), (bf16[512,256]{1,0:T(8,128)(2,1)}, bf16[512,256]{1,0:T(8,128)(2,1)})) %all-reduce.6.cloned.1.call-update) | async-done | bytes 524304 | tf_op jit(solution)/shard_map/psum | solution.py:109
  280.4 11.8 %fusion.44 = f32[512,2048]{1,0:T(8,128)S(1)} fusion(bf16[512,256]{1,0:T(8,128)(2,1)} %get-tuple-element.5, s32[256]{0:T(256)S(1)} %copy-done.6, s32[2048]{0:T(1024)S(1)} %add_select_fusion.9, s32[256]{0:T(256)S(1)} %copy-done.8), kind=kOutput, calls=%fused_computation.77 | convolution fusion | flops 550502400 | bytes 4466688 | tf_op jit(solution)/shard_map/dot_general | solution.py:25
  292.1 12.3 %multiply_convert_fusion = bf16[512,2048]{1,0:T(8,128)(2,1)} fusion(f32[512,2048]{1,0:T(8,128)S(1)} %fusion.44, bf16[512,256]{1,0:T(8,128)(2,1)S(1)} %copy-done.10, f32[2048]{0:T(1024)S(1)} %copy-done.12, s32[256]{0:T(256)S(1)} %copy-done.6, s32[2048]{0:T(1024)S(1)} %add_select_fusion.9, s32[256]{0:T(256)S(1)} %copy-done.8), kind=kOutput, calls=%fused_computation | convolution fusion | flops 553648128 | bytes 6572032 | tf_op jit(solution)/shard_map/dot_general | solution.py:25
  (54 shorter events, 2.8 us)
Async XLA Ops:
  6.5 2.8 copy-start
  6.5 103.3 %reduce-scatter.2.cloned.1.call-start = ((), (), s32[]{:S(2)}) async-start(), calls=%async_computation.3 | async-start | bytes 1310720 | tf_op jit(solution)/shard_map/reduce_scatter | solution.py:65
  8.6 13.6 %copy-start.5 = (s32[256]{0:T(256)}, s32[256]{0:T(256)S(1)}, u32[]{:S(2)}) copy-start(s32[256]{0:T(256)S(1)} %get-tuple-element.14) | copy-start | bytes 3076
  8.6 13.6 %copy-start.7 = (s32[256]{0:T(256)}, s32[256]{0:T(256)S(1)}, u32[]{:S(2)}) copy-start(s32[256]{0:T(256)S(1)} %get-tuple-element.15) | copy-start | bytes 3076
  9.3 12.9 %copy-start.11 = (f32[2048]{0:T(1024)S(1)}, f32[2048]{0:T(1024)}, u32[]{:S(2)}) copy-start(f32[2048]{0:T(1024)} %param.8) | copy-start | bytes 24580
  22.3 11.1 %copy-start.13 = (s32[8]{0:T(128)S(1)}, s32[8]{0:T(128)}, u32[]{:S(2)}) copy-start(s32[8]{0:T(128)} %param.10) | copy-start | bytes 100
  33.4 33.1 %copy-start.3 = (s32[512]{0:T(512)}, s32[512]{0:T(512)S(1)}, u32[]{:S(2)}) copy-start(s32[512]{0:T(512)S(1)} %add_select_fusion.16) | copy-start | bytes 6148
  33.6 10.6 %copy-start.14 = (bf16[256,512]{1,0:T(8,128)(2,1)S(1)}, bf16[256,512]{1,0:T(8,128)(2,1)}, u32[]{:S(2)}) copy-start(bf16[256,512]{1,0:T(8,128)(2,1)} %convolution_convert_fusion.3) | copy-start | bytes 786436
  78.6 75.8 %copy-start.1 = (bf16[256,256]{1,0:T(8,128)(2,1)S(1)}, bf16[256,256]{1,0:T(8,128)(2,1)}, u32[]{:S(2)}) copy-start(bf16[256,256]{1,0:T(8,128)(2,1)} %param.12) | copy-start | bytes 393220
  79.7 82.0 %copy-start.2 = (s32[8,16,16]{2,1,0:T(8,128)S(1)}, s32[8,16,16]{2,1,0:T(8,128)}, u32[]{:S(2)}) copy-start(s32[8,16,16]{2,1,0:T(8,128)} %param.13) | copy-start | bytes 24580
  79.7 74.7 %all-reduce.4.cloned.1.call-start = ((), (), s32[]{:S(2)}) async-start(), calls=%async_computation.4 | async-start | bytes 524288 | tf_op jit(solution)/shard_map/psum | solution.py:68
  157.0 15.4 %all-to-all-start = ((bf16[4,2,16384]{2,1,0:T(2,128)(2,1)}), bf16[4,2,16384]{2,1,0:T(2,128)(2,1)S(1)}, u32[]{:S(2)}, u32[]{:S(2)}) async-start(bf16[4,2,16384]{2,1,0:T(2,128)(2,1)} %reshape.290), calls=%async_computation.1 | async-start | bytes 524288 | tf_op jit(solution)/shard_map/all_to_all | solution.py:83
  161.6 55.1 %all-gather.2.cloned.1.call-start = ((), (), s32[]{:S(2)}) async-start(), calls=%async_computation.5 | async-start | bytes 1310720 | tf_op jit(solution)/shard_map/all_gather | solution.py:98
  175.7 41.1 %copy-start.4 = (s32[512]{0:T(512)S(1)}, s32[512]{0:T(512)}, u32[]{:S(2)}) copy-start(s32[512]{0:T(512)} %copy-done.3) | copy-start | bytes 6148
  190.5 89.9 %all-reduce.6.cloned.1.call-start = ((), (), s32[]{:S(2)}) async-start(), calls=%async_computation.6 | async-start | bytes 1048576 | tf_op jit(solution)/shard_map/psum | solution.py:109
  216.7 11.7 %copy-start.9 = (bf16[2,4,256,256]{3,2,1,0:T(8,128)(2,1)S(1)}, bf16[2,4,256,256]{3,2,1,0:T(8,128)(2,1)}, u32[]{:S(2)}) copy-start(bf16[2,4,256,256]{3,2,1,0:T(8,128)(2,1)} %all-gather.2.cloned.1.call-done) | copy-start | bytes 3145732
  250.7 29.6 %copy-start.6 = (s32[256]{0:T(256)S(1)}, s32[256]{0:T(256)}, u32[]{:S(2)}) copy-start(s32[256]{0:T(256)} %copy-done.5) | copy-start | bytes 3076
  250.7 29.6 %copy-start.8 = (s32[256]{0:T(256)S(1)}, s32[256]{0:T(256)}, u32[]{:S(2)}) copy-start(s32[256]{0:T(256)} %copy-done.7) | copy-start | bytes 3076
  280.3 11.8 %copy-start.10 = (bf16[512,256]{1,0:T(8,128)(2,1)S(1)}, bf16[512,256]{1,0:T(8,128)(2,1)}, u32[]{:S(2)}) copy-start(bf16[512,256]{1,0:T(8,128)(2,1)} %get-tuple-element.6) | copy-start | bytes 786436
  280.3 11.8 %copy-start.12 = (f32[2048]{0:T(1024)S(1)}, f32[2048]{0:T(1024)}, u32[]{:S(2)}) copy-start(f32[2048]{0:T(1024)} %param.8) | copy-start | bytes 24580
Sparse Core Ops, SparseCore 0:
  79.8 29.9 reduce-scatter.1
  112.8 41.5 all-reduce.3
  190.6 26.0 all-gather.1
  262.3 18.0 all-reduce.5
where the time goes:
time: 316 us; the launch traced here: 311 us
  matrix products  141 us (45%)
  waiting for transfers between devices  119 us (38%)
  local copies, waits for them, and re-layouts  17.5 us (6%)
  between operations  15.1 us (5%)
  blocking collectives  12.7 us (4%)
  starting transfers between devices  4.85 us (2%)
    dot_general x6, matrix products, product(): return jnp.dot(left, right, preferred_element_type=jnp.float32)  69 us
    psum x1, waiting for transfers between devices, body(): blocks = lax.psum(blocks, 'facet')  44.5 us
    reduce_scatter x1, waiting for transfers between devices, body(): lax.psum_scatter(terms.astype(jnp.bfloat16), 'band', scatter_dimension=2,...  30.1 us
    all_gather x1, waiting for transfers between devices, body(): piece = lax.all_gather(residual_grid, 'band', axis=2, tiled=True)  26 us
    psum x1, waiting for transfers between devices, body(): lax.psum(e_real.astype(jnp.bfloat16), 'sub').astype(jnp.float32)  18.2 us
    dot_general x1, matrix products, body(): jnp.einsum('xy,ky->xk', facets, col_imag, preferred_element_type=jnp.floa...  12.9 us
    all_to_all x1, blocking collectives, body(): lax.all_to_all(u_cols, 'band', split_axis=3, concat_axis=2, tiled=True)  12.7 us
    dot_general x1, matrix products, body(): jnp.einsum('gkx,gkl->xl', back_imag, piece[0], preferred_element_type=jnp...  11.7 us
  transfers between devices with their start and end apart: 5, of which 4 were waited for; matrix products, arithmetic and copies ran while one was open for 3% of the time, Pallas kernels for 0%

commit v1 on v0

--- a/solution.py
+++ b/solution.py
@@ -65,7 +65,12 @@
     blocks = lax.psum_scatter(
         terms.astype(jnp.bfloat16), "band", scatter_dimension=2, tiled=True
     ).astype(jnp.float32)
-    blocks = lax.psum(blocks, "facet")
+    size = lax.axis_size("facet")
+    total, hop = (blocks, 1)
+    while hop < size:
+        total = total + lax.ppermute(total, "facet", [(i, i ^ hop) for i in range(size)])
+        hop = 2 * hop
+    blocks = total
     grid_part = blocks.reshape(2, band_count, sub_rows, contrib).astype(jnp.bfloat16)
     tiles = tile_counts.shape[1]
     tile_side = contrib // tiles

time: 316 us -> 298 us (0.943)
  waiting for transfers between devices: 119 us -> 98.2 us
    psum x1 -> x0, waiting for transfers between devices: 44.5 us -> none  [body(): blocks = lax.psum(blocks, 'facet')]
    ppermute x0 -> x2, waiting for transfers between devices: none -> 22.8 us  [body(): lax.ppermute(total, 'facet', [(i, i ^ hop) for i in range(size)])]
  transfers between devices with their start and end apart: 5 -> 6, of which waited for: 4 -> 5; matrix products, arithmetic and copies ran while one was open for 3% -> 4% of each run, Pallas kernels for 0% -> 0%
where the time goes in v1:
time: 298 us; the launch traced here: 293 us
  matrix products  140 us (47%)
  waiting for transfers between devices  98.2 us (33%)
  local copies, waits for them, and re-layouts  17.6 us (6%)
  between operations  15.2 us (5%)
  blocking collectives  11.9 us (4%)
  starting transfers between devices  6.75 us (2%)
    dot_general x6, matrix products, product(): return jnp.dot(left, right, preferred_element_type=jnp.float32)  69 us
    reduce_scatter x1, waiting for transfers between devices, body(): lax.psum_scatter(terms.astype(jnp.bfloat16), 'band', scatter_dimension=2,...  30.2 us
    all_gather x1, waiting for transfers between devices, body(): piece = lax.all_gather(residual_grid, 'band', axis=2, tiled=True)  27.1 us
    ppermute x2, waiting for transfers between devices, body(): lax.ppermute(total, 'facet', [(i, i ^ hop) for i in range(size)])  22.8 us
    psum x1, waiting for transfers between devices, body(): lax.psum(e_real.astype(jnp.bfloat16), 'sub').astype(jnp.float32)  18.2 us
    dot_general x1, matrix products, body(): jnp.einsum('xy,ky->xk', facets, col_imag, preferred_element_type=jnp.floa...  12.9 us
    all_to_all x1, blocking collectives, body(): lax.all_to_all(u_cols, 'band', split_axis=3, concat_axis=2, tiled=True)  11.9 us
    dot_general x1, matrix products, body(): jnp.einsum('gkx,gkl->xl', back_imag, piece[0], preferred_element_type=jnp...  11.7 us
  transfers between devices with their start and end apart: 6, of which 5 were waited for; matrix products, arithmetic and copies ran while one was open for 4% of the time, Pallas kernels for 0%

profile of v1, /device:TPU:0, one launch (start us, length us, event | category | flops | bytes accessed | tf_op | source)
XLA Modules:
  0.0 293.0 jit_solution(7507359886808642962)
XLA Ops:
  7.3 0.8 constant_dynamic-slice_fusion
  8.7 0.7 add_select_fusion.9
  9.4 12.9 %convolution_convert_fusion.3 = bf16[256,512]{1,0:T(8,128)(2,1)} fusion(bf16[512,2048]{1,0:T(8,128)(2,1)S(1)} %copy-done, f32[2048]{0:T(1024)} %param.8, s32[256]{0:T(256)S(1)} %get-tuple-element.14, s32[2048]{0:T(1024)S(1)} %add_select_fusion.9, s32[256]{0:T(256)S(1)} %get-tuple-element.15), kind=kOutput, calls=%fused_computation.73 | convolution fusion | flops 551682048 | bytes 2377728 | tf_op jit(solution)/shard_map/xy,ky->xk/dot_general | solution.py:53
  22.3 10.5 %convolution_convert_fusion.4 = bf16[256,512]{1,0:T(8,128)(2,1)S(1)} fusion(bf16[512,2048]{1,0:T(8,128)(2,1)S(1)} %copy-done, f32[2048]{0:T(1024)S(1)} %copy-done.11, s32[256]{0:T(256)S(1)} %get-tuple-element.14, s32[2048]{0:T(1024)S(1)} %add_select_fusion.9, s32[256]{0:T(256)S(1)} %get-tuple-element.15), kind=kOutput, calls=%fused_computation.74 | convolution fusion | flops 551157760 | bytes 2377728 | tf_op jit(solution)/shard_map/xy,ky->xk/dot_general | solution.py:50
  33.8 10.6 %fusion.58 = f32[1024,256]{1,0:T(8,128)S(1)} fusion(bf16[256,512]{1,0:T(8,128)(2,1)S(1)} %convolution_convert_fusion.4, s32[1024]{0:T(1024)S(1)} %get-tuple-element.8, s32[512]{0:T(512)S(1)} %add_select_fusion.16, s32[1024]{0:T(1024)S(1)} %get-tuple-element.7), kind=kOutput, calls=%fused_computation.88 | convolution fusion | flops 282066944 | bytes 1320960 | tf_op jit(solution)/shard_map/dot_general | solution.py:25
  44.4 10.7 %fusion.57 = f32[1024,256]{1,0:T(8,128)S(1)} fusion(bf16[256,512]{1,0:T(8,128)(2,1)S(1)} %copy-done.14, s32[1024]{0:T(1024)S(1)} %get-tuple-element.8, s32[512]{0:T(512)S(1)} %add_select_fusion.16, s32[1024]{0:T(1024)S(1)} %get-tuple-element.7), kind=kOutput, calls=%fused_computation.87 | convolution fusion | flops 282066944 | bytes 1320960 | tf_op jit(solution)/shard_map/dot_general | solution.py:25
  55.1 11.6 %fusion.36 = bf16[1024,256]{1,0:T(8,128)(2,1)S(1)} fusion(f32[1024,256]{1,0:T(8,128)S(1)} %fusion.58, bf16[256,512]{1,0:T(8,128)(2,1)S(1)} %copy-done.14, s32[1024]{0:T(1024)S(1)} %get-tuple-element.8, s32[512]{0:T(512)S(1)} %add_select_fusion.16, s32[1024]{0:T(1024)S(1)} %get-tuple-element.7), kind=kOutput, calls=%fused_computation.59 | convolution fusion | flops 283115520 | bytes 1845248 | tf_op jit(solution)/shard_map/dot_general | solution.py:25
  66.7 12.0 %fusion.37 = bf16[1024,256]{1,0:T(8,128)(2,1)S(1)} fusion(f32[1024,256]{1,0:T(8,128)S(1)} %fusion.57, bf16[256,512]{1,0:T(8,128)(2,1)S(1)} %convolution_convert_fusion.4, s32[1024]{0:T(1024)S(1)} %get-tuple-element.8, s32[512]{0:T(512)S(1)} %add_select_fusion.16, s32[1024]{0:T(1024)S(1)} %get-tuple-element.7), kind=kOutput, calls=%fused_computation.60 | convolution fusion | flops 283115520 | bytes 1845248 | tf_op jit(solution)/shard_map/dot_general | solution.py:25
  78.8 1.0 copy.25
  79.9 30.2 %reduce-scatter.2.cloned.1.call-done = bf16[2,4,1,64,256]{4,3,1,0,2:T(8,128)(2,1)} async-done(((bf16[2,4,4,64,256]{4,3,1,0,2:T(8,128)(2,1)}), bf16[2,4,1,64,256]{4,3,1,0,2:T(8,128)(2,1)}) %reduce-scatter.2.cloned.1.call-update) | async-done | bytes 262160 | tf_op jit(solution)/shard_map/reduce_scatter | solution.py:65
  110.0 1.0 convert_element_type.115
  111.0 1.5 collective-permute-start
  112.6 11.8 %collective-permute-done = f32[2,4,1,64,256]{4,3,1,0,2:T(8,128)S(1)} collective-permute-done((f32[2,4,1,64,256]{4,3,1,0,2:T(8,128)S(1)}, f32[2,4,1,64,256]{4,3,1,0,2:T(8,128)S(1)}, u32[]{:S(2)}, u32[]{:S(2)}) %collective-permute-start) | collective-permute-done | bytes 524320 | tf_op jit(solution)/shard_map/ppermute | solution.py:71
  124.4 1.0 convert_add_fusion
  125.4 1.5 collective-permute-start.1
  126.9 11.0 %collective-permute-done.1 = f32[2,4,1,64,256]{4,3,1,0,2:T(8,128)S(1)} collective-permute-done((f32[2,4,1,64,256]{4,3,1,0,2:T(8,128)S(1)}, f32[2,4,1,64,256]{4,3,1,0,2:T(8,128)S(1)}, u32[]{:S(2)}, u32[]{:S(2)}) %collective-permute-start.1) | collective-permute-done | bytes 524320 | tf_op jit(solution)/shard_map/ppermute | solution.py:71
  138.5 1.1 reshape.290
  139.6 3.4 %all-to-all-start = ((bf16[4,2,16384]{2,1,0:T(2,128)(2,1)}), bf16[4,2,16384]{2,1,0:T(2,128)(2,1)S(1)}, u32[]{:S(2)}, u32[]{:S(2)}) async-start(bf16[4,2,16384]{2,1,0:T(2,128)(2,1)} %reshape.290), calls=%async_computation.1 | async-start | bytes 524288 | tf_op jit(solution)/shard_map/all_to_all | solution.py:88
  143.2 3.9 %broadcast_in_dim.2 = f32[4,16,16,16,16]{2,1,4,3,0:T(8,128)} broadcast(f32[4,16,16]{1,2,0:T(8,128)S(1)} %copy.17), dimensions={0,1,3} | broadcast | bytes 1052672 | tf_op jit(solution)/shard_map/broadcast_in_dim | solution.py:81
  147.1 6.1 %reshape.284 = f32[4,256,256]{1,2,0:T(8,128)S(1)} reshape(f32[4,16,16,16,16]{2,1,4,3,0:T(8,128)} %broadcast_in_dim.2) | data formatting | bytes 2097152 | tf_op jit(solution)/shard_map/reshape | solution.py:84
  153.2 0.7 dynamic-slice_bitcast_fusion
  155.0 1.4 convolution_convert_fusion.1
  157.2 11.9 %all_to_all.36 = bf16[4,2,16384]{2,1,0:T(2,128)(2,1)S(1)} all-to-all(bf16[4,2,16384]{2,1,0:T(2,128)(2,1)S(1)} %reshape.292), channel_id=1, replica_groups=mesh['facet'=4,'band'=4,'sub'=2] {'band'}, dimensions={0} | all-to-all | bytes 524288 | tf_op jit(solution)/shard_map/all_to_all | solution.py:97
  170.2 0.9 convolution_convert_fusion
  171.4 27.1 %all-gather.2.cloned.1.call-done = bf16[2,4,256,256]{3,2,1,0:T(8,128)(2,1)} async-done(((bf16[2,4,64,256]{3,2,1,0:T(8,128)(2,1)}), bf16[2,4,256,256]{3,2,1,0:T(8,128)(2,1)}) %all-gather.2.cloned.1.call-update) | async-done | bytes 1048592 | tf_op jit(solution)/shard_map/all_gather | solution.py:103
  198.4 11.7 %convolution_bitcast_fusion = f32[512,256]{1,0:T(8,128)S(1)} fusion(s32[4,256]{1,0:T(4,128)S(1)} %get-tuple-element.12, s32[512]{0:T(512)S(1)} %copy-done.4, s32[4,256]{1,0:T(4,128)S(1)} %get-tuple-element.13, bf16[2,4,256,256]{3,2,1,0:T(8,128)(2,1)} %all-gather.2.cloned.1.call-done), kind=kOutput, calls=%fused_computation.61 | convolution fusion | flops 282066944 | bytes 1058816 | tf_op jit(solution)/shard_map/gkx,gkl->xl/dot_general | solution.py:109
  210.1 10.7 %convolution_bitcast_fusion.2 = f32[512,256]{1,0:T(8,128)S(1)} fusion(s32[4,256]{1,0:T(4,128)S(1)} %get-tuple-element.12, s32[512]{0:T(512)S(1)} %copy-done.4, s32[4,256]{1,0:T(4,128)S(1)} %get-tuple-element.13, bf16[2,4,256,256]{3,2,1,0:T(8,128)(2,1)S(1)} %copy-done.9), kind=kOutput, calls=%fused_computation.63 | convolution fusion | flops 282066944 | bytes 1058816 | tf_op jit(solution)/shard_map/gkx,gkl->xl/dot_general | solution.py:105
  220.9 11.6 %fusion.40 = bf16[512,256]{1,0:T(8,128)(2,1)} fusion(f32[512,256]{1,0:T(8,128)S(1)} %convolution_bitcast_fusion, s32[4,256]{1,0:T(4,128)S(1)} %get-tuple-element.12, s32[512]{0:T(512)S(1)} %copy-done.4, s32[4,256]{1,0:T(4,128)S(1)} %get-tuple-element.13, bf16[2,4,256,256]{3,2,1,0:T(8,128)(2,1)S(1)} %copy-done.9), kind=kOutput, calls=%fused_computation.68 | convolution fusion | flops 282329088 | bytes 1320960 | tf_op jit(solution)/shard_map/gkx,gkl->xl/dot_general | solution.py:108
  232.5 11.4 %fusion.41 = bf16[512,256]{1,0:T(8,128)(2,1)} fusion(f32[512,256]{1,0:T(8,128)S(1)} %convolution_bitcast_fusion.2, s32[4,256]{1,0:T(4,128)S(1)} %get-tuple-element.12, s32[512]{0:T(512)S(1)} %copy-done.4, s32[4,256]{1,0:T(4,128)S(1)} %get-tuple-element.13, bf16[2,4,256,256]{3,2,1,0:T(8,128)(2,1)S(1)} %copy-done.9), kind=kOutput, calls=%fused_computation.69 | convolution fusion | flops 282329088 | bytes 1320960 | tf_op jit(solution)/shard_map/gkx,gkl->xl/dot_general | solution.py:104
  243.9 18.2 %all-reduce.3.cloned.1.call-done = (bf16[512,256]{1,0:T(8,128)(2,1)}, bf16[512,256]{1,0:T(8,128)(2,1)}) async-done(((bf16[512,256]{1,0:T(8,128)(2,1)}, bf16[512,256]{1,0:T(8,128)(2,1)}), (bf16[512,256]{1,0:T(8,128)(2,1)}, bf16[512,256]{1,0:T(8,128)(2,1)})) %all-reduce.3.cloned.1.call-update) | async-done | bytes 524304 | tf_op jit(solution)/shard_map/psum | solution.py:114
  262.1 11.8 %fusion.44 = f32[512,2048]{1,0:T(8,128)S(1)} fusion(bf16[512,256]{1,0:T(8,128)(2,1)} %get-tuple-element.5, s32[256]{0:T(256)S(1)} %copy-done.6, s32[2048]{0:T(1024)S(1)} %add_select_fusion.9, s32[256]{0:T(256)S(1)} %copy-done.8), kind=kOutput, calls=%fused_computation.77 | convolution fusion | flops 550502400 | bytes 4466688 | tf_op jit(solution)/shard_map/dot_general | solution.py:25
  273.8 12.3 %multiply_convert_fusion = bf16[512,2048]{1,0:T(8,128)(2,1)} fusion(f32[512,2048]{1,0:T(8,128)S(1)} %fusion.44, bf16[512,256]{1,0:T(8,128)(2,1)S(1)} %copy-done.10, f32[2048]{0:T(1024)S(1)} %copy-done.12, s32[256]{0:T(256)S(1)} %copy-done.6, s32[2048]{0:T(1024)S(1)} %add_select_fusion.9, s32[256]{0:T(256)S(1)} %copy-done.8), kind=kOutput, calls=%fused_computation | convolution fusion | flops 553648128 | bytes 6572032 | tf_op jit(solution)/shard_map/dot_general | solution.py:25
  (57 shorter events, 4.9 us)
Async XLA Ops:
  6.5 2.9 copy-start
  6.5 103.5 %reduce-scatter.2.cloned.1.call-start = ((), (), s32[]{:S(2)}) async-start(), calls=%async_computation.3 | async-start | bytes 1310720 | tf_op jit(solution)/shard_map/reduce_scatter | solution.py:65
  8.7 13.6 %copy-start.5 = (s32[256]{0:T(256)}, s32[256]{0:T(256)S(1)}, u32[]{:S(2)}) copy-start(s32[256]{0:T(256)S(1)} %get-tuple-element.14) | copy-start | bytes 3076
  8.7 13.6 %copy-start.7 = (s32[256]{0:T(256)}, s32[256]{0:T(256)S(1)}, u32[]{:S(2)}) copy-start(s32[256]{0:T(256)S(1)} %get-tuple-element.15) | copy-start | bytes 3076
  9.4 12.9 %copy-start.11 = (f32[2048]{0:T(1024)S(1)}, f32[2048]{0:T(1024)}, u32[]{:S(2)}) copy-start(f32[2048]{0:T(1024)} %param.8) | copy-start | bytes 24580
  22.3 11.2 %copy-start.13 = (s32[8]{0:T(128)S(1)}, s32[8]{0:T(128)}, u32[]{:S(2)}) copy-start(s32[8]{0:T(128)} %param.10) | copy-start | bytes 100
  33.5 33.1 %copy-start.3 = (s32[512]{0:T(512)}, s32[512]{0:T(512)S(1)}, u32[]{:S(2)}) copy-start(s32[512]{0:T(512)S(1)} %add_select_fusion.16) | copy-start | bytes 6148
  33.8 10.6 %copy-start.14 = (bf16[256,512]{1,0:T(8,128)(2,1)S(1)}, bf16[256,512]{1,0:T(8,128)(2,1)}, u32[]{:S(2)}) copy-start(bf16[256,512]{1,0:T(8,128)(2,1)} %convolution_convert_fusion.3) | copy-start | bytes 786436
  79.9 58.1 %copy-start.1 = (bf16[256,256]{1,0:T(8,128)(2,1)S(1)}, bf16[256,256]{1,0:T(8,128)(2,1)}, u32[]{:S(2)}) copy-start(bf16[256,256]{1,0:T(8,128)(2,1)} %param.12) | copy-start | bytes 393220
  111.0 13.4 %collective-permute-start = (f32[2,4,1,64,256]{4,3,1,0,2:T(8,128)S(1)}, f32[2,4,1,64,256]{4,3,1,0,2:T(8,128)S(1)}, u32[]{:S(2)}, u32[]{:S(2)}) collective-permute-start(f32[2,4,1,64,256]{4,3,1,0,2:T(8,128)S(1)} %convert_element_type.115), channel_id=1, source_target_pairs={{0,8},{8,0},{16,24},{24,16},{1,9},{9,1},{17,25},{25,17},{2,10},{10... | collective-permute-start | bytes 1572872 | tf_op jit(solution)/shard_map/ppermute | solution.py:71
  125.4 17.7 %copy-start.2 = (s32[8,16,16]{2,1,0:T(8,128)S(1)}, s32[8,16,16]{2,1,0:T(8,128)}, u32[]{:S(2)}) copy-start(s32[8,16,16]{2,1,0:T(8,128)} %param.13) | copy-start | bytes 24580
  125.4 12.5 %collective-permute-start.1 = (f32[2,4,1,64,256]{4,3,1,0,2:T(8,128)S(1)}, f32[2,4,1,64,256]{4,3,1,0,2:T(8,128)S(1)}, u32[]{:S(2)}, u32[]{:S(2)}) collective-permute-start(f32[2,4,1,64,256]{4,3,1,0,2:T(8,128)S(1)} %convert_add_fusion), channel_id=1, source_target_pairs={{0,16},{8,24},{16,0},{24,8},{1,17},{9,25},{17,1},{25,9},{2,18},{10... | collective-permute-start | bytes 1572872 | tf_op jit(solution)/shard_map/ppermute | solution.py:71
  139.6 14.3 %all-to-all-start = ((bf16[4,2,16384]{2,1,0:T(2,128)(2,1)}), bf16[4,2,16384]{2,1,0:T(2,128)(2,1)S(1)}, u32[]{:S(2)}, u32[]{:S(2)}) async-start(bf16[4,2,16384]{2,1,0:T(2,128)(2,1)} %reshape.290), calls=%async_computation.1 | async-start | bytes 524288 | tf_op jit(solution)/shard_map/all_to_all | solution.py:88
  143.0 55.4 %all-gather.2.cloned.1.call-start = ((), (), s32[]{:S(2)}) async-start(), calls=%async_computation.4 | async-start | bytes 1310720 | tf_op jit(solution)/shard_map/all_gather | solution.py:103
  157.1 41.3 %copy-start.4 = (s32[512]{0:T(512)S(1)}, s32[512]{0:T(512)}, u32[]{:S(2)}) copy-start(s32[512]{0:T(512)} %copy-done.3) | copy-start | bytes 6148
  171.1 90.9 %all-reduce.3.cloned.1.call-start = ((), (), s32[]{:S(2)}) async-start(), calls=%async_computation.5 | async-start | bytes 1048576 | tf_op jit(solution)/shard_map/psum | solution.py:114
  198.4 11.7 %copy-start.9 = (bf16[2,4,256,256]{3,2,1,0:T(8,128)(2,1)S(1)}, bf16[2,4,256,256]{3,2,1,0:T(8,128)(2,1)}, u32[]{:S(2)}) copy-start(bf16[2,4,256,256]{3,2,1,0:T(8,128)(2,1)} %all-gather.2.cloned.1.call-done) | copy-start | bytes 3145732
  232.5 29.6 %copy-start.6 = (s32[256]{0:T(256)S(1)}, s32[256]{0:T(256)}, u32[]{:S(2)}) copy-start(s32[256]{0:T(256)} %copy-done.5) | copy-start | bytes 3076
  232.5 29.6 %copy-start.8 = (s32[256]{0:T(256)S(1)}, s32[256]{0:T(256)}, u32[]{:S(2)}) copy-start(s32[256]{0:T(256)} %copy-done.7) | copy-start | bytes 3076
  262.1 11.8 %copy-start.10 = (bf16[512,256]{1,0:T(8,128)(2,1)S(1)}, bf16[512,256]{1,0:T(8,128)(2,1)}, u32[]{:S(2)}) copy-start(bf16[512,256]{1,0:T(8,128)(2,1)} %get-tuple-element.6) | copy-start | bytes 786436
  262.1 11.8 %copy-start.12 = (f32[2048]{0:T(1024)S(1)}, f32[2048]{0:T(1024)}, u32[]{:S(2)}) copy-start(f32[2048]{0:T(1024)} %param.8) | copy-start | bytes 24580
Sparse Core Ops, SparseCore 0:
  80.0 29.9 reduce-scatter.1
  171.3 27.1 all-gather.1
  244.0 18.0 all-reduce.2
